TPU v7x, 256 devices: a whole 4x4x8 slice. The times are simulated.
256 devices in a mesh: dap: 128 (over x_lo, y, z, core), dp: 2 (over x_hi).
Axes of the slice: x: 4 (x_hi: 2, x_lo: 2; x = x_hi * 2 + x_lo), y: 4, z: 8, core: 2. Of those that a mesh axis runs over, the one named last changes fastest.
Arguments:
- alignment_embedding: bfloat16 [256, 128, 256], P('dp', 'dap'), parts along dimension 0, may hold values from -6 to 6
- alignment_existing_flags: int32 [256, 128], P('dp', 'dap'), parts along dimension 0, may hold values 0 or 1
- couple_embedding: bfloat16 [256, 128, 128], P(('dp', 'dap')), parts along dimension 0, may hold values from -6 to 6
- alignment_scaling_factor: float32 [256], replicated, may hold values from 0.1 to 1.9
- couple_scaling_factor: float32 [128], replicated, may hold values from 0.1 to 1.9
- request_matrix: bfloat16 [256, 256], replicated, may hold values from -0.375 to 0.375
- lookup_matrix: bfloat16 [256, 256], replicated, may hold values from -0.375 to 0.375
- content_matrix: bfloat16 [256, 256], replicated, may hold values from -0.375 to 0.375
- switch_matrix: bfloat16 [256, 256], replicated, may hold values from -0.375 to 0.375
- final_projection_matrix: bfloat16 [256, 256], replicated, may hold values from -0.375 to 0.375
- couple_to_headterm_matrix: bfloat16 [128, 8], replicated, may hold values from -30 to 30
- increment_adjoint: bfloat16 [256, 128, 256], P('dp', 'dap'), parts along dimension 0, may hold values from -48 to 48
Outputs:
- alignment_increment: bfloat16 [256, 128, 256], P('dp', 'dap'), parts along dimension 0
- alignment_adjoint: bfloat16 [256, 128, 256], P('dp', 'dap'), parts along dimension 0
- couple_adjoint: bfloat16 [256, 128, 128], P(('dp', 'dap')), parts along dimension 0
- d_w_query: float32 [512, 256], P('dp'), parts along dimension 0
- d_w_key: float32 [512, 256], P('dp'), parts along dimension 0
- d_w_value: float32 [512, 256], P('dp'), parts along dimension 0
- d_w_gate: float32 [512, 256], P('dp'), parts along dimension 0
- d_w_out: float32 [512, 256], P('dp'), parts along dimension 0
- couple_headterm_adjoint: float32 [256, 8], P('dp'), parts along dimension 0
- d_msa_gain: float32 [512], P('dp'), parts along dimension 0
- couple_scaling_adjoint: float32 [256], P('dp'), parts along dimension 0
There are 2 independent parts, one for each index of `dp`. A program takes and returns all parts, laid end to end along the dimension named above; an argument that names none is the same for every part. Nothing has to cross between parts.
All inputs are finite; a program needn't handle non-finite values. No bound on the sum of `alignment_existing_flags` on one device may be relied on, other than what follows from the above.
Results may differ from a plain program's by a relative error of at most 0.012.
The roundings to bfloat16 on the way count: a program that leaves them out, or rounds other values in their place, can miss the bound.
Values may be sent and summed in bfloat16 or wider, within the bound.
No kernel may reach another device: no remote copies, remote signals or barrier semaphores. Data moves between devices by JAX's collectives and lax.ppermute only.
A program may use at most 64 MiB of HBM per device.

v0:
```python
import jax
import jax.numpy as jnp
from jax import lax
from jax.sharding import PartitionSpec as P

ALIGN_FEATURES = 256
HEAD_NUMBER = 8
HEAD_DIMENSION = 32
EPS = 1e-05


def standardise_features(value, gain):
    mean = jnp.mean(value, axis=-1, keepdims=True)
    centered = value - mean
    variance = jnp.mean(centered * centered, axis=-1, keepdims=True)
    reciprocal_spread = lax.rsqrt(variance + EPS)
    standardised_lines = centered * reciprocal_spread
    return (standardised_lines, reciprocal_spread, standardised_lines * gain)


def standardise_features_adjoint(upstream_gradient, standardised_lines, reciprocal_spread, gain):
    rescaled_request = upstream_gradient * gain
    return reciprocal_spread * (
        rescaled_request
        - jnp.mean(rescaled_request, axis=-1, keepdims=True)
        - standardised_lines
        * jnp.mean(rescaled_request * standardised_lines, axis=-1, keepdims=True)
    )


def tensor_product(left, right):
    return lax.dot_general(
        left, right, (((0,), (0,)), ((), ())), preferred_element_type=jnp.float32
    )


def onward_one_line(
    alignment_line_content,
    line_filter_flags,
    couple_headwise_terms,
    alignment_scaling_factor,
    request_matrix,
    lookup_matrix,
    content_matrix,
    switch_matrix,
    final_projection_matrix,
):
    element_number = alignment_line_content.shape[0]
    standardised_lines, reciprocal_spread, rescaled_request = standardise_features(
        alignment_line_content.astype(jnp.float32), alignment_scaling_factor
    )
    input_arrays = rescaled_request.astype(jnp.bfloat16)
    query = (
        jnp.dot(input_arrays, request_matrix, preferred_element_type=jnp.float32)
        * HEAD_DIMENSION ** (-0.5)
    ).astype(jnp.bfloat16)
    keys = jnp.dot(input_arrays, lookup_matrix, preferred_element_type=jnp.float32).astype(
        jnp.bfloat16
    )
    values = jnp.dot(input_arrays, content_matrix, preferred_element_type=jnp.float32).astype(
        jnp.bfloat16
    )
    gate_sigmoid = jax.nn.sigmoid(
        jnp.dot(input_arrays, switch_matrix, preferred_element_type=jnp.float32)
    )
    query = query.reshape(element_number, HEAD_NUMBER, HEAD_DIMENSION)
    keys = keys.reshape(element_number, HEAD_NUMBER, HEAD_DIMENSION)
    values = values.reshape(element_number, HEAD_NUMBER, HEAD_DIMENSION)
    scores = jnp.einsum("ihd,jhd->ihj", query, keys, preferred_element_type=jnp.float32)
    scores = (
        scores
        + couple_headwise_terms.astype(jnp.float32)
        + (1000000000.0 * (line_filter_flags.astype(jnp.float32) - 1.0))[None, None, :]
    )
    probs = jax.nn.softmax(scores, axis=-1)
    probs_low = probs.astype(jnp.bfloat16)
    attention_probs = jnp.einsum(
        "ihj,jhd->ihd", probs_low, values, preferred_element_type=jnp.float32
    ).reshape(element_number, HEAD_NUMBER * HEAD_DIMENSION)
    weighted_values = (gate_sigmoid * attention_probs).astype(jnp.bfloat16)
    alignment_increment = jnp.dot(
        weighted_values, final_projection_matrix, preferred_element_type=jnp.float32
    ).astype(jnp.bfloat16)
    kept_intermediates = (
        standardised_lines,
        reciprocal_spread,
        input_arrays,
        query,
        keys,
        values,
        gate_sigmoid,
        attention_probs,
        weighted_values,
        probs,
    )
    return (alignment_increment, kept_intermediates)


def reverse_one_line(
    line_adjoint_routine,
    kept_intermediates,
    alignment_scaling_factor,
    request_matrix,
    lookup_matrix,
    content_matrix,
    switch_matrix,
    final_projection_matrix,
):
    (
        standardised_lines,
        reciprocal_spread,
        input_arrays,
        query,
        keys,
        values,
        gate_sigmoid,
        attention_probs,
        weighted_values,
        probs,
    ) = kept_intermediates
    element_number = line_adjoint_routine.shape[0]
    probs_low = probs.astype(jnp.bfloat16)
    upstream_gradient = lax.dot_general(
        line_adjoint_routine,
        final_projection_matrix,
        (((1,), (1,)), ((), ())),
        preferred_element_type=jnp.float32,
    )
    d_attn = (upstream_gradient * gate_sigmoid).astype(jnp.bfloat16)
    gate_logit_gradient = (
        upstream_gradient * attention_probs * gate_sigmoid * (1.0 - gate_sigmoid)
    ).astype(jnp.bfloat16)
    d_attn_heads = d_attn.reshape(element_number, HEAD_NUMBER, HEAD_DIMENSION)
    d_probs = jnp.einsum("ihd,jhd->ihj", d_attn_heads, values, preferred_element_type=jnp.float32)
    affinity_adjoint = probs * (d_probs - jnp.sum(probs * d_probs, axis=-1, keepdims=True))
    d_low = affinity_adjoint.astype(jnp.bfloat16)
    query_gradient = (
        (
            jnp.einsum("ihj,jhd->ihd", d_low, keys, preferred_element_type=jnp.float32)
            * HEAD_DIMENSION ** (-0.5)
        )
        .astype(jnp.bfloat16)
        .reshape(element_number, HEAD_NUMBER * HEAD_DIMENSION)
    )
    key_gradient = (
        jnp.einsum("ihj,ihd->jhd", d_low, query, preferred_element_type=jnp.float32)
        .astype(jnp.bfloat16)
        .reshape(element_number, HEAD_NUMBER * HEAD_DIMENSION)
    )
    value_gradient = (
        jnp.einsum("ihj,ihd->jhd", probs_low, d_attn_heads, preferred_element_type=jnp.float32)
        .astype(jnp.bfloat16)
        .reshape(element_number, HEAD_NUMBER * HEAD_DIMENSION)
    )
    backward_result = (((1,), (1,)), ((), ()))
    argument_adjoints = lax.dot_general(
        query_gradient, request_matrix, backward_result, preferred_element_type=jnp.float32
    )
    argument_adjoints = argument_adjoints + lax.dot_general(
        key_gradient, lookup_matrix, backward_result, preferred_element_type=jnp.float32
    )
    argument_adjoints = argument_adjoints + lax.dot_general(
        value_gradient, content_matrix, backward_result, preferred_element_type=jnp.float32
    )
    argument_adjoints = argument_adjoints + lax.dot_general(
        gate_logit_gradient, switch_matrix, backward_result, preferred_element_type=jnp.float32
    )
    line_adjoint = standardise_features_adjoint(
        argument_adjoints, standardised_lines, reciprocal_spread, alignment_scaling_factor
    ).astype(jnp.bfloat16)
    matrix_adjoints = (
        tensor_product(input_arrays, query_gradient),
        tensor_product(input_arrays, key_gradient),
        tensor_product(input_arrays, value_gradient),
        tensor_product(input_arrays, gate_logit_gradient),
        tensor_product(weighted_values, line_adjoint_routine),
        jnp.sum(argument_adjoints * standardised_lines, axis=0),
    )
    return (line_adjoint, affinity_adjoint, matrix_adjoints)


def on_device(
    alignment_embedding,
    alignment_existing_flags,
    couple_embedding,
    alignment_scaling_factor,
    couple_scaling_factor,
    request_matrix,
    lookup_matrix,
    content_matrix,
    switch_matrix,
    final_projection_matrix,
    couple_to_headterm_matrix,
    increment_adjoint,
):
    filter_shared = alignment_existing_flags.astype(jnp.bfloat16)
    alignment_line_embedding, alignment_line_flags = (
        lax.all_to_all(alignment_embedding, "dap", split_axis=0, concat_axis=1, tiled=True),
        lax.all_to_all(filter_shared, "dap", split_axis=0, concat_axis=1, tiled=True),
    )
    pair_hat, pair_inv, pair_scaled = standardise_features(
        couple_embedding.astype(jnp.float32), couple_scaling_factor
    )
    pair_ln = pair_scaled.astype(jnp.bfloat16)
    bias_rows = jnp.einsum(
        "ijc,ch->ihj", pair_ln, couple_to_headterm_matrix, preferred_element_type=jnp.float32
    ).astype(jnp.bfloat16)
    couple_headwise_terms = lax.all_gather(bias_rows, "dap", axis=0, tiled=True)

    def onward_loop_step(carry, loop_elements):
        alignment_increment, kept_intermediates = onward_one_line(
            loop_elements[0],
            loop_elements[1],
            couple_headwise_terms,
            alignment_scaling_factor,
            request_matrix,
            lookup_matrix,
            content_matrix,
            switch_matrix,
            final_projection_matrix,
        )
        return (carry, (alignment_increment, kept_intermediates))

    unused_value, (row_updates, all_saved_residuals) = lax.scan(
        onward_loop_step, None, (alignment_line_embedding, alignment_line_flags)
    )
    update_out = lax.all_to_all(row_updates, "dap", split_axis=1, concat_axis=0, tiled=True)
    seq_grad = lax.all_to_all(increment_adjoint, "dap", split_axis=0, concat_axis=1, tiled=True)
    amino_positions = alignment_line_embedding.shape[1]
    span_length = HEAD_NUMBER * HEAD_DIMENSION
    blank_matrix = (
        jnp.zeros((ALIGN_FEATURES, span_length), jnp.float32),
        jnp.zeros((ALIGN_FEATURES, span_length), jnp.float32),
        jnp.zeros((ALIGN_FEATURES, span_length), jnp.float32),
        jnp.zeros((ALIGN_FEATURES, span_length), jnp.float32),
        jnp.zeros((span_length, ALIGN_FEATURES), jnp.float32),
        jnp.zeros((ALIGN_FEATURES,), jnp.float32),
    )

    def backward_step(carry, loop_elements):
        bias_sum, subtotal_list = carry
        line_adjoint, affinity_adjoint, matrix_adjoints = reverse_one_line(
            loop_elements[0],
            loop_elements[1],
            alignment_scaling_factor,
            request_matrix,
            lookup_matrix,
            content_matrix,
            switch_matrix,
            final_projection_matrix,
        )
        subtotal_list = tuple((a + b for a, b in zip(subtotal_list, matrix_adjoints)))
        return ((bias_sum + affinity_adjoint, subtotal_list), line_adjoint)

    beginning_shift = (
        jnp.zeros((amino_positions, HEAD_NUMBER, amino_positions), jnp.float32),
        blank_matrix,
    )
    (bias_term, subtotal_list), line_adjoint_list = lax.scan(
        backward_step, beginning_shift, (seq_grad, all_saved_residuals)
    )
    additive_term_adjoint = lax.psum_scatter(bias_term, "dap", scatter_dimension=0, tiled=True)
    d_pln = jnp.einsum(
        "ihj,ch->ijc",
        additive_term_adjoint,
        couple_to_headterm_matrix.astype(jnp.float32),
        precision=lax.Precision.HIGHEST,
    )
    w_bias_part = jnp.einsum(
        "ijc,ihj->ch",
        pair_ln.astype(jnp.float32),
        additive_term_adjoint,
        precision=lax.Precision.HIGHEST,
    )
    pair_gain_part = jnp.sum(d_pln * pair_hat, axis=(0, 1))
    couple_adjoint = standardise_features_adjoint(
        d_pln, pair_hat, pair_inv, couple_scaling_factor
    ).astype(jnp.bfloat16)
    totals = lax.psum(
        (
            subtotal_list[0],
            subtotal_list[1],
            subtotal_list[2],
            subtotal_list[3],
            subtotal_list[4],
            w_bias_part,
            subtotal_list[5],
            pair_gain_part,
        ),
        "dap",
    )
    alignment_adjoint = lax.all_to_all(
        line_adjoint_list, "dap", split_axis=1, concat_axis=0, tiled=True
    )
    return (
        update_out,
        alignment_adjoint,
        couple_adjoint,
        totals[0],
        totals[1],
        totals[2],
        totals[3],
        totals[4],
        totals[5],
        totals[6],
        totals[7],
    )


def solution(mesh):
    in_specs = (
        P("dp", "dap", None),
        P("dp", "dap"),
        P(("dp", "dap"), None, None),
        P(),
        P(),
        P(),
        P(),
        P(),
        P(),
        P(),
        P(),
        P("dp", "dap", None),
    )
    out_specs = (
        P("dp", "dap", None),
        P("dp", "dap", None),
        P(("dp", "dap"), None, None),
        P("dp", None),
        P("dp", None),
        P("dp", None),
        P("dp", None),
        P("dp", None),
        P("dp", None),
        P("dp"),
        P("dp"),
    )
    return jax.shard_map(
        on_device, mesh=mesh, in_specs=in_specs, out_specs=out_specs, check_vma=False
    )
```

profile of v0, /device:TPU:4, one launch (start us, length us, event | category | flops | bytes accessed | tf_op | source)
XLA Modules:
  0.0 1600.0 jit_solution(11764958021694046716)
XLA Ops:
  7.2 0.7 convert_bitcast_fusion.2
  7.9 0.8 copy.78
  8.7 14.1 all-to-all-start.1
  23.0 0.6 copy-done.15
  23.8 157.6 %all-gather = bf16[1024,128]{1,0:T(8,128)(2,1)S(1)} all-gather(bf16[8,128]{1,0:T(8,128)(2,1)S(1)} %fusion.11), channel_id=2, replica_groups=mesh['dap'=128,'dp'=2] {'dap'}, dimensions={0}, use_global_device_ids=true | all-gather | bytes 264192 | tf_op jit(solution)/shard_map/all_gather | solution.py:208
  181.4 0.5 broadcast.220
  182.0 0.7 reduce.9
  182.6 0.7 reshape.335
  183.3 6.1 all-to-all-start
  189.5 0.8 copy-done.11
  190.3 0.7 reduce.8
  190.9 0.7 reshape.339
  191.6 0.2 copy.77
  191.8 1.0 multiply_reduce_fusion.2
  192.9 6.9 all-to-all-done
  199.7 6.1 all-to-all-start.3
  206.3 0.6 copy-done.8
  207.0 0.2 convolution_convert_fusion.4
  207.3 0.8 copy-done.7
  208.1 0.2 convolution_convert_fusion.3
  208.5 0.8 copy-done.9
  209.3 0.2 fusion.9
  209.6 0.3 fusion.4
  209.9 0.5 fusion.75
  210.4 0.2 fusion.33
  210.7 5.5 all-to-all-done.3
  216.4 0.3 multiply_convert_fusion
  216.8 0.3 multiply_reduce_fusion
  217.4 0.2 convolution_convert_fusion.1
  217.6 0.3 convolution_convert_fusion
  217.9 1.0 copy.89
  218.9 1.0 fusion.67
  219.9 1.0 fusion.65
  220.9 1.0 fusion.63
  221.9 1.0 fusion.69
  222.9 0.9 fusion.50
  224.2 1.0 reduce.10
  225.2 0.7 reshape.337
  225.8 8.0 all-to-all-start.2
  234.0 0.2 convolution_add_fusion.2
  234.5 0.3 fusion.24
  235.0 1.0 reduce.11
  236.1 0.6 reshape.341
  236.7 7.6 all-to-all-done.2
  244.3 6.1 all-to-all-start.4
  250.4 0.7 copy-done.16
  251.0 0.6 dynamic-slice.6
  251.7 0.6 copy.112
  252.3 8.6 all-to-all-done.4
  260.9 0.6 copy.111
  261.5 1041.0 %all-reduce.5.cloned.1.call-done = (f32[128,8,128]{2,1,0:T(8,128)}, f32[256,256]{1,0:T(8,128)}, f32[256,256]{1,0:T(8,128)}, f32[256,256]{1,0:T(8,128)}, f32[256,256]{1,0:T(8,128)}, /*index=5*/f32[256,256]{1,0:T(8,128)}) async-done(((f32[128,8,128]{2,1,0:T(8,128)}, f32[256,256]{1,0:T(8,128)}, f32[256,256]{1,0:T(8,128)}, f32[256,256]{1,0:T(8,128)}, f32[256,256]{1,0:T(8,128)}, ...) | async-done | bytes 1835024
  1302.6 1.7 fusion.46
  1304.3 1.5 fusion.57
  1306.1 0.7 copy.90
  1306.8 281.5 %all-reduce.1 = (f32[128,8]{0,1:T(8,128)}, f32[256]{0:T(256)}, f32[128]{0:T(128)}) all-reduce(f32[128,8]{0,1:T(8,128)S(1)} %fusion.57, f32[256]{0:T(256)S(1)} %get-tuple-element.196, f32[128]{0:T(128)S(1)} %get-tuple-element.199), channel_id=1, replica_groups=mesh['dap'=128,'dp'=2] {'dap'}, use_global_device_ids=true, to_apply=%region_17.18 | all-reduce | flops 1408 | bytes 11264 | tf_op jit(solution)/shard_map/psum | solution.py:279
  1588.3 0.7 copy.123
  1589.0 0.3 copy-done.5
  1589.3 0.7 copy.124
  1590.0 0.3 copy-done.4
  1590.4 0.7 copy.125
  1591.1 0.3 copy-done.3
  1591.4 0.7 copy.126
  1592.1 0.3 copy-done.2
  1592.4 0.7 copy.127
  (60 shorter events, 3.2 us)
Async XLA Ops:
  7.2 209.3 %copy-start = (bf16[256,256]{1,0:T(8,128)(2,1)S(1)}, bf16[256,256]{1,0:T(8,128)(2,1)}, u32[]{:S(2)}) copy-start(bf16[256,256]{1,0:T(8,128)(2,1)} %param.20) | copy-start | bytes 393220
  8.7 14.1 copy-start.13
  8.7 174.6 %all-to-all-start.1 = ((bf16[128,1,1]{2,1,0:T(2,128)(2,1)}), bf16[128,1,1]{2,1,0:T(2,128)(2,1)S(1)}, u32[]{:S(2)}, u32[]{:S(2)}) async-start(bf16[128,1,1]{2,1,0:T(2,128)(2,1)} %copy.78), calls=%async_computation.1 | async-start | bytes 131072 | tf_op jit(solution)/shard_map/all_to_all | solution.py:199
  22.9 0.7 copy-start.15
  23.0 0.7 copy-start.14
  23.8 158.1 %copy-start.10 = (bf16[128,1,256]{2,0,1:T(8,128)(2,1)S(1)}, bf16[128,1,256]{2,0,1:T(8,128)(2,1)}, u32[]{:S(2)}) copy-start(bf16[128,1,256]{2,0,1:T(8,128)(2,1)} %param.12) | copy-start | bytes 196612
  183.3 16.5 %all-to-all-start = ((bf16[128,2,128]{2,1,0:T(2,128)(2,1)}), bf16[128,2,128]{2,1,0:T(2,128)(2,1)S(1)}, u32[]{:S(2)}, u32[]{:S(2)}) async-start(bf16[128,2,128]{2,1,0:T(2,128)(2,1)} %reshape.335), calls=%async_computation | async-start | bytes 131072 | tf_op jit(solution)/shard_map/all_to_all | solution.py:198
  189.4 0.8 copy-start.11
  199.7 16.5 %all-to-all-start.3 = ((bf16[128,2,128]{2,1,0:T(2,128)(2,1)}), bf16[128,2,128]{2,1,0:T(2,128)(2,1)S(1)}, u32[]{:S(2)}, u32[]{:S(2)}) async-start(bf16[128,2,128]{2,1,0:T(2,128)(2,1)} %reshape.339), calls=%async_computation.3 | async-start | bytes 131072 | tf_op jit(solution)/shard_map/all_to_all | solution.py:228
  205.9 1096.7 %all-reduce.5.cloned.1.call-start = ((), (), s32[]{:S(2)}) async-start(), calls=%async_computation.5 | async-start | bytes 3670016
  206.0 0.9 copy-start.8
  206.3 0.7 copy-start.12
  207.2 0.9 copy-start.7
  208.3 0.9 copy-start.9
  210.7 5.5 copy-start.1
  225.8 18.4 %all-to-all-start.2 = ((bf16[128,2,128]{2,1,0:T(2,128)(2,1)}), bf16[128,2,128]{2,1,0:T(2,128)(2,1)S(1)}, u32[]{:S(2)}, u32[]{:S(2)}) async-start(bf16[128,2,128]{2,1,0:T(2,128)(2,1)} %reshape.337), calls=%async_computation.2 | async-start | bytes 131072 | tf_op jit(solution)/shard_map/all_to_all | solution.py:227
  244.3 16.6 %all-to-all-start.4 = ((bf16[128,2,128]{2,1,0:T(2,128)(2,1)}), bf16[128,2,128]{2,1,0:T(2,128)(2,1)S(1)}, u32[]{:S(2)}, u32[]{:S(2)}) async-start(bf16[128,2,128]{2,1,0:T(2,128)(2,1)} %reshape.341), calls=%async_computation.4 | async-start | bytes 131072 | tf_op jit(solution)/shard_map/all_to_all | solution.py:292
  250.4 0.7 copy-start.16
  1302.6 285.7 %copy-start.6 = (f32[256,256]{1,0:T(8,128)S(1)}, f32[256,256]{1,0:T(8,128)}, u32[]{:S(2)}) copy-start(f32[256,256]{1,0:T(8,128)} %get-tuple-element.228) | copy-start | bytes 786436
  1588.3 1.0 copy-start.5
  1589.3 1.0 copy-start.4
  1590.4 1.0 copy-start.3
  1591.4 1.0 copy-start.2
Sparse Core Ops, SparseCore 0:
  224.0 1078.5 all-reduce.4
where the time goes:
time: 1600 us
  waiting for transfers between devices  1070 us (67%)
  blocking collectives  439 us (27%)
  starting transfers between devices  40.5 us (3%)
  local copies, waits for them, and re-layouts  18 us (1%)
    unnamed x2, waiting for transfers between devices  1040 us
    psum x1, blocking collectives, on_device(): lax.psum((subtotal_list[0], subtotal_list[1], subtotal_list[2], subtotal_...  281 us
    all_gather x1, blocking collectives, on_device(): couple_headwise_terms = lax.all_gather(bias_rows, 'dap', axis=0, tiled=True)  158 us
  transfers between devices with their start and end apart: 6, of which 5 were waited for; matrix products, arithmetic and copies ran while one was open for 1% of the time, Pallas kernels for 0%

commit v1 on v0

--- a/solution.py
+++ b/solution.py
@@ -205,7 +205,9 @@
     bias_rows = jnp.einsum(
         "ijc,ch->ihj", pair_ln, couple_to_headterm_matrix, preferred_element_type=jnp.float32
     ).astype(jnp.bfloat16)
-    couple_headwise_terms = lax.all_gather(bias_rows, "dap", axis=0, tiled=True)
+    couple_headwise_terms = jnp.concatenate(
+        lax.all_to_all(jnp.stack([bias_rows] * lax.axis_size("dap")), "dap", 0, 0), axis=0
+    )
 
     def onward_loop_step(carry, loop_elements):
         alignment_increment, kept_intermediates = onward_one_line(

time: 1600 us -> 1470 us (0.919)
  blocking collectives: 439 us -> 281 us
  waiting for transfers between devices: 1070 us -> 1090 us
    all_gather x1 -> x0, blocking collectives: 158 us -> none  [on_device(): couple_headwise_terms = lax.all_gather(bias_rows, 'dap', axis=0, tiled=True)]
  transfers between devices with their start and end apart: 6 -> 7, of which waited for: 5 -> 7; matrix products, arithmetic and copies ran while one was open for 1% -> 1% of each run, Pallas kernels for 0% -> 0%
where the time goes in v1:
time: 1470 us
  waiting for transfers between devices  1090 us (74%)
  blocking collectives  281 us (19%)
  starting transfers between devices  45.7 us (3%)
  local copies, waits for them, and re-layouts  18 us (1%)
    unnamed x2, waiting for transfers between devices  1040 us
    psum x1, blocking collectives, on_device(): lax.psum((subtotal_list[0], subtotal_list[1], subtotal_list[2], subtotal_...  281 us
  transfers between devices with their start and end apart: 7, of which 7 were waited for; matrix products, arithmetic and copies ran while one was open for 1% of the time, Pallas kernels for 0%

profile of v1, /device:TPU:4, one launch (start us, length us, event | category | flops | bytes accessed | tf_op | source)
XLA Modules:
  0.0 1470.8 jit_solution(9994232051850191990)
XLA Ops:
  7.2 0.7 convert_bitcast_fusion.2
  7.9 0.8 copy.77
  8.7 14.1 all-to-all-start.2
  23.0 0.5 broadcast.222
  23.6 0.7 reduce.9
  24.3 0.7 reshape.340
  24.9 8.1 all-to-all-done.2
  33.1 6.1 all-to-all-start
  39.4 0.6 copy-done.11
  40.1 0.7 reduce.8
  40.7 0.7 reshape.344
  41.4 1.0 multiply_reduce_fusion.2
  42.4 7.1 all-to-all-done
  49.5 6.1 all-to-all-start.4
  56.1 0.6 copy-done.8
  56.9 9.0 all-to-all-done.4
  66.0 0.7 stack.2
  66.7 6.3 all-to-all-start.1
  73.0 0.2 all-reduce.5.cloned.1.call-start
  73.3 0.2 convolution_convert_fusion.3
  73.7 0.7 copy-done.9
  74.4 0.2 fusion.9
  74.8 0.9 copy-done.1
  75.9 10.1 all-to-all-done.1
  85.9 0.2 copy.76
  86.2 0.4 fusion.75
  86.6 0.5 fusion.33
  87.2 0.3 multiply_convert_fusion
  87.6 0.3 multiply_reduce_fusion
  88.1 0.2 convolution_convert_fusion.1
  88.3 0.5 convolution_convert_fusion
  88.9 1.0 copy.88
  89.9 1.0 fusion.67
  90.9 1.0 fusion.65
  91.9 1.0 fusion.63
  92.9 1.0 fusion.69
  93.9 0.9 fusion.50
  95.1 1.0 reduce.10
  96.2 0.7 reshape.342
  96.8 6.7 all-to-all-start.3
  104.2 0.3 fusion.24
  104.7 1.0 reduce.11
  105.8 0.6 reshape.346
  106.4 7.5 all-to-all-done.3
  113.9 6.1 all-to-all-start.5
  120.0 0.7 copy-done.16
  120.6 0.6 dynamic-slice.6
  121.3 0.6 copy.111
  121.9 8.4 all-to-all-done.5
  130.3 0.6 copy.110
  131.0 1042.4 %all-reduce.5.cloned.1.call-done = (f32[128,8,128]{2,1,0:T(8,128)}, f32[256,256]{1,0:T(8,128)}, f32[256,256]{1,0:T(8,128)}, f32[256,256]{1,0:T(8,128)}, f32[256,256]{1,0:T(8,128)}, /*index=5*/f32[256,256]{1,0:T(8,128)}) async-done(((f32[128,8,128]{2,1,0:T(8,128)}, f32[256,256]{1,0:T(8,128)}, f32[256,256]{1,0:T(8,128)}, f32[256,256]{1,0:T(8,128)}, f32[256,256]{1,0:T(8,128)}, ...) | async-done | bytes 1835024
  1173.4 1.7 fusion.46
  1175.1 1.5 fusion.57
  1176.9 0.7 copy.89
  1177.6 281.5 %all-reduce.1 = (f32[128,8]{0,1:T(8,128)}, f32[256]{0:T(256)}, f32[128]{0:T(128)}) all-reduce(f32[128,8]{0,1:T(8,128)S(1)} %fusion.57, f32[256]{0:T(256)S(1)} %get-tuple-element.196, f32[128]{0:T(128)S(1)} %get-tuple-element.199), channel_id=1, replica_groups=mesh['dap'=128,'dp'=2] {'dap'}, use_global_device_ids=true, to_apply=%region_17.18 | all-reduce | flops 1408 | bytes 11264 | tf_op jit(solution)/shard_map/psum | solution.py:281
  1459.1 0.7 copy.122
  1459.8 0.3 copy-done.5
  1460.1 0.7 copy.123
  1460.8 0.3 copy-done.4
  1461.2 0.7 copy.124
  1461.9 0.3 copy-done.3
  1462.2 0.7 copy.125
  1462.9 0.3 copy-done.2
  1463.3 0.7 copy.126
  (60 shorter events, 3.6 us)
Async XLA Ops:
  7.2 80.0 %copy-start = (bf16[256,256]{1,0:T(8,128)(2,1)S(1)}, bf16[256,256]{1,0:T(8,128)(2,1)}, u32[]{:S(2)}) copy-start(bf16[256,256]{1,0:T(8,128)(2,1)} %param.20) | copy-start | bytes 393220
  8.7 14.1 copy-start.13
  8.7 24.4 %all-to-all-start.2 = ((bf16[128,1,1]{2,1,0:T(2,128)(2,1)}), bf16[128,1,1]{2,1,0:T(2,128)(2,1)S(1)}, u32[]{:S(2)}, u32[]{:S(2)}) async-start(bf16[128,1,1]{2,1,0:T(2,128)(2,1)} %copy.77), calls=%async_computation.2 | async-start | bytes 131072 | tf_op jit(solution)/shard_map/all_to_all | solution.py:199
  22.8 0.8 copy-start.10
  24.9 14.3 copy-start.14
  24.9 14.3 copy-start.15
  33.1 16.5 %all-to-all-start = ((bf16[128,2,128]{2,1,0:T(2,128)(2,1)}), bf16[128,2,128]{2,1,0:T(2,128)(2,1)S(1)}, u32[]{:S(2)}, u32[]{:S(2)}) async-start(bf16[128,2,128]{2,1,0:T(2,128)(2,1)} %reshape.340), calls=%async_computation | async-start | bytes 131072 | tf_op jit(solution)/shard_map/all_to_all | solution.py:198
  39.2 0.8 copy-start.11
  49.5 16.5 %all-to-all-start.4 = ((bf16[128,2,128]{2,1,0:T(2,128)(2,1)}), bf16[128,2,128]{2,1,0:T(2,128)(2,1)S(1)}, u32[]{:S(2)}, u32[]{:S(2)}) async-start(bf16[128,2,128]{2,1,0:T(2,128)(2,1)} %reshape.344), calls=%async_computation.4 | async-start | bytes 131072 | tf_op jit(solution)/shard_map/all_to_all | solution.py:230
  55.7 0.9 copy-start.8
  56.0 0.7 copy-start.12
  66.7 6.5 copy-start.7
  66.7 19.2 %all-to-all-start.1 = ((bf16[128,1,8,128]{3,2,1,0:T(8,128)(2,1)}), bf16[128,1,8,128]{3,2,1,0:T(8,128)(2,1)S(1)}, u32[]{:S(2)}, u32[]{:S(2)}) async-start(bf16[128,1,8,128]{3,2,1,0:T(8,128)(2,1)} %stack.2), calls=%async_computation.1 | async-start | bytes 524288 | tf_op jit(solution)/shard_map/all_to_all | solution.py:209
  73.0 1100.4 %all-reduce.5.cloned.1.call-start = ((), (), s32[]{:S(2)}) async-start(), calls=%async_computation.6 | async-start | bytes 3670016
  73.5 0.9 copy-start.9
  74.8 0.9 copy-start.1
  96.8 17.1 %all-to-all-start.3 = ((bf16[128,2,128]{2,1,0:T(2,128)(2,1)}), bf16[128,2,128]{2,1,0:T(2,128)(2,1)S(1)}, u32[]{:S(2)}, u32[]{:S(2)}) async-start(bf16[128,2,128]{2,1,0:T(2,128)(2,1)} %reshape.342), calls=%async_computation.3 | async-start | bytes 131072 | tf_op jit(solution)/shard_map/all_to_all | solution.py:229
  113.9 16.4 %all-to-all-start.5 = ((bf16[128,2,128]{2,1,0:T(2,128)(2,1)}), bf16[128,2,128]{2,1,0:T(2,128)(2,1)S(1)}, u32[]{:S(2)}, u32[]{:S(2)}) async-start(bf16[128,2,128]{2,1,0:T(2,128)(2,1)} %reshape.346), calls=%async_computation.5 | async-start | bytes 131072 | tf_op jit(solution)/shard_map/all_to_all | solution.py:294
  120.0 0.7 copy-start.16
  1173.4 285.7 %copy-start.6 = (f32[256,256]{1,0:T(8,128)S(1)}, f32[256,256]{1,0:T(8,128)}, u32[]{:S(2)}) copy-start(f32[256,256]{1,0:T(8,128)} %get-tuple-element.228) | copy-start | bytes 786436
  1459.1 1.0 copy-start.5
  1460.1 1.0 copy-start.4
  1461.2 1.0 copy-start.3
  1462.2 1.0 copy-start.2
Sparse Core Ops, SparseCore 0:
  95.0 1078.3 all-reduce.4
